TPU v7x, 32 devices: a whole 2x2x4 slice. The times are simulated.
32 devices in a mesh: dp: 8 (over y, x, core), ctx: 4 (over z).
Axes of the slice: x: 2, y: 2, z: 4, core: 2. Of those that a mesh axis runs over, the one named last changes fastest.
Arguments:
- tokens: bfloat16 [8, 2048, 960], P('dp', 'ctx'), may hold values from -6 to 6
- cotangent: bfloat16 [8, 2048, 960], P('dp', 'ctx'), may hold values from -6 to 6
- lengths: int32 [8], P('dp'), may hold values from 512 to 2048, as said below
- gate_mask: int32 [8, 2048], P('dp', 'ctx'), may hold values 0 or 1
- block_order: int32 [8], replicated, may hold values from 0 to 7, as said below
- w_query: bfloat16 [921600], P(('dp', 'ctx')), may hold values from -0.1875 to 0.1875
- w_key: bfloat16 [307200], P(('dp', 'ctx')), may hold values from -0.1875 to 0.1875
- w_value: bfloat16 [307200], P(('dp', 'ctx')), may hold values from -0.1875 to 0.1875
- w_out: bfloat16 [921600], P(('dp', 'ctx')), may hold values from -1.5 to 1.5
- w_gate: bfloat16 [2457600], P(('dp', 'ctx')), may hold values from -0.1875 to 0.1875
- w_up: bfloat16 [2457600], P(('dp', 'ctx')), may hold values from -0.1875 to 0.1875
- w_down: bfloat16 [2457600], P(('dp', 'ctx')), may hold values from -0.125 to 0.125
- gain_attn: float32 [960], replicated, may hold values from 0.5 to 1.5
- gain_mlp: float32 [960], replicated, may hold values from 0.5 to 1.5
- w_router: float32 [960], replicated, may hold values from -0.1875 to 0.1875
Outputs:
- out_tokens: bfloat16 [8, 2048, 960], P('dp', 'ctx')
- grad_tokens: bfloat16 [8, 2048, 960], P('dp', 'ctx')
- grad_query: float32 [921600], P(('dp', 'ctx'))
- grad_key: float32 [307200], P(('dp', 'ctx'))
- grad_value: float32 [307200], P(('dp', 'ctx'))
- grad_out: float32 [921600], P(('dp', 'ctx'))
- grad_gate: float32 [2457600], P(('dp', 'ctx'))
- grad_up: float32 [2457600], P(('dp', 'ctx'))
- grad_down: float32 [2457600], P(('dp', 'ctx'))
- grad_gain_attn: float32 [960], replicated
- grad_gain_mlp: float32 [960], replicated
- grad_router: float32 [960], replicated
Inputs may be any that keep to these rules, and one draw needn't show every extreme that they name: `lengths`: every sequence has between 512 and 2048 valid tokens; some sequence has exactly 2048 and some exactly 512. `block_order`: stored blocks 2 c and 2 c + 1 hold causal blocks k and 7 - k, in either order; every causal block appears once.
All inputs are finite; a program needn't handle non-finite values. No bound on the sum of `gate_mask` on one device may be relied on, other than what follows from the above.
Results may differ from a plain program's by a relative error of at most 0.014.
Values may be sent and summed in bfloat16 or wider, within the bound.
No kernel may reach another device: no remote copies, remote signals or barrier semaphores. Data moves between devices by JAX's collectives and lax.ppermute only.
A program may use at most 192 MiB of HBM per device.

v0:
```python
import jax
import jax.numpy as jnp
from jax import lax
from jax.sharding import PartitionSpec as P

HEADS = 15
KV_HEADS = 5
HEAD_DIM = 64
FF = 2560
norm_eps = 1e-05
rope_base = 100000.0
neg_big = -1e30
highest = lax.Precision.HIGHEST


def rms_norm(values_in, gain_vec):
    return (
        values_in
        * lax.rsqrt(jnp.mean(values_in * values_in, axis=-1, keepdims=True) + norm_eps)
        * gain_vec
    )


def rotary(positions, head_width):
    frequency = rope_base ** (-jnp.arange(0, head_width, 2).astype(jnp.float32) / head_width)
    angles = positions.astype(jnp.float32)[:, None] * frequency[None, :]
    return (jnp.cos(angles)[:, None, :], jnp.sin(angles)[:, None, :])


def rotate(tensor, cosine, sine_table):
    half_width = tensor.shape[-1] // 2
    first_half = tensor[..., :half_width]
    second = tensor[..., half_width:]
    return jnp.concatenate(
        [first_half * cosine - second * sine_table, second * cosine + first_half * sine_table],
        axis=-1,
    )


def matmul(left, right):
    return jnp.dot(left, right, preferred_element_type=jnp.float32)


def matmul_left_t(left, right):
    return lax.dot_general(
        left, right, (((0,), (0,)), ((), ())), preferred_element_type=jnp.float32
    )


def matmul_right_t(left, right):
    return lax.dot_general(
        left, right, (((1,), (1,)), ((), ())), preferred_element_type=jnp.float32
    )


def silu_times(gate_proj, up_proj):
    return jax.nn.silu(gate_proj) * up_proj


def per_device(
    tokens,
    cotangent,
    lengths,
    gate_mask,
    block_order,
    w_query,
    w_key,
    w_value,
    w_out,
    w_gate,
    w_up,
    w_down,
    gain_attn,
    gain_mlp,
    w_router,
):
    inputs = tokens[0].astype(jnp.float32)
    row_count = inputs.shape[0]
    model_width = inputs.shape[1]
    head_count = HEADS
    kv_count = KV_HEADS
    head_width = HEAD_DIM
    group_size = head_count // kv_count
    kv_width = kv_count * head_width
    ff_width = FF
    score_scale = head_width ** (-0.5)
    ctx_index = lax.axis_index("ctx")
    block_rows = row_count // 2
    all_pos = (
        block_order[:, None] * block_rows + jnp.arange(block_rows, dtype=jnp.int32)[None, :]
    ).reshape(-1)
    total_rows = all_pos.shape[0]
    own_pos = lax.dynamic_slice_in_dim(all_pos, ctx_index * row_count, row_count)
    seq_length = lengths[0]
    allowed = (all_pos[None, :] <= own_pos[:, None]) & (all_pos < seq_length)[None, :]
    targets = (
        (model_width, model_width),
        (model_width, kv_width),
        (model_width, kv_width),
        (model_width, model_width),
        (model_width, ff_width),
        (model_width, ff_width),
        (ff_width, model_width),
    )
    whole = (
        lax.all_gather(w_query, ("dp", "ctx"), axis=0, tiled=True),
        lax.all_gather(w_key, ("dp", "ctx"), axis=0, tiled=True),
        lax.all_gather(w_value, ("dp", "ctx"), axis=0, tiled=True),
        lax.all_gather(w_out, ("dp", "ctx"), axis=0, tiled=True),
        lax.all_gather(w_gate, ("dp", "ctx"), axis=0, tiled=True),
        lax.all_gather(w_up, ("dp", "ctx"), axis=0, tiled=True),
        lax.all_gather(w_down, ("dp", "ctx"), axis=0, tiled=True),
    )
    weight_query, weight_key, weight_value, weight_out, weight_gate, weight_up, weight_down = tuple(
        (flat_piece.reshape(target) for flat_piece, target in zip(whole, targets))
    )
    cosine, sine_table = rotary(own_pos, head_width)
    normed, norm_back = jax.vjp(rms_norm, inputs, gain_attn)
    normed_b = normed.astype(jnp.bfloat16)
    queries = rotate(
        matmul(normed_b, weight_query).reshape(row_count, head_count, head_width),
        cosine,
        sine_table,
    ).astype(jnp.bfloat16)
    key_local = (
        rotate(
            matmul(normed_b, weight_key).reshape(row_count, kv_count, head_width),
            cosine,
            sine_table,
        )
        .astype(jnp.bfloat16)
        .reshape(row_count, kv_width)
    )
    value_local = matmul(normed_b, weight_value).astype(jnp.bfloat16)
    key_all, value_all = (
        lax.all_gather(key_local, "ctx", axis=0, tiled=True),
        lax.all_gather(value_local, "ctx", axis=0, tiled=True),
    )
    query_heads = queries.reshape(row_count, kv_count, group_size, head_width).transpose(1, 0, 2, 3)

    def split_heads(flat_rows):
        return flat_rows.reshape(total_rows, kv_count, head_width).transpose(1, 0, 2)

    def head_forward(packed):
        query_head, key_head, value_head = packed
        raw_scores = (
            jnp.einsum("qgd,kd->gqk", query_head, key_head, preferred_element_type=jnp.float32)
            * score_scale
        )
        raw_scores = jnp.where(allowed[None], raw_scores, neg_big)
        top_score = jnp.max(raw_scores, axis=-1, keepdims=True)
        expo = jnp.exp(raw_scores - top_score)
        totals = jnp.sum(expo, axis=-1, keepdims=True)
        probs = (expo / totals).astype(jnp.bfloat16)
        head_out = jnp.einsum("gqk,kd->qgd", probs, value_head, preferred_element_type=jnp.float32)
        return (head_out, top_score[..., 0] + jnp.log(totals[..., 0]))

    head_outs, log_totals = lax.map(
        head_forward, (query_heads, split_heads(key_all), split_heads(value_all))
    )
    mixed_b = head_outs.transpose(1, 0, 2, 3).reshape(row_count, model_width).astype(jnp.bfloat16)
    attn_out = matmul(mixed_b, weight_out)
    middle = inputs + attn_out
    normed_mlp, mlp_norm_back = jax.vjp(rms_norm, middle, gain_mlp)
    normed_mlp_b = normed_mlp.astype(jnp.bfloat16)
    gate_proj = matmul(normed_mlp_b, weight_gate)
    up_proj = matmul(normed_mlp_b, weight_up)
    hidden_f, silu_back = jax.vjp(silu_times, gate_proj, up_proj)
    hidden = hidden_f.astype(jnp.bfloat16)
    mlp_out = matmul(hidden, weight_down)
    branch = attn_out + mlp_out
    router_gate = jax.nn.sigmoid(jnp.dot(inputs, w_router, precision=highest))
    gate_bits = gate_mask[0].astype(jnp.float32)
    chosen = gate_bits * router_gate
    result = (inputs + chosen[:, None] * branch).astype(jnp.bfloat16)
    usable = (own_pos < seq_length).astype(jnp.float32)
    grad_result = cotangent[0].astype(jnp.float32) * usable[:, None]
    grad_branch = grad_result * chosen[:, None]
    grad_logit = (
        gate_bits * jnp.sum(grad_result * branch, axis=-1) * router_gate * (1.0 - router_gate)
    )
    grad_router = jnp.dot(grad_logit, inputs, precision=highest)
    grad_inputs = grad_result + grad_logit[:, None] * w_router[None, :]
    grad_mlp_b = grad_branch.astype(jnp.bfloat16)
    grad_w_down = matmul_left_t(hidden, grad_mlp_b)
    grad_hidden = matmul_right_t(grad_mlp_b, weight_down)
    grad_gate_f, grad_up_f = silu_back(grad_hidden)
    grad_gate_b = grad_gate_f.astype(jnp.bfloat16)
    grad_up_b = grad_up_f.astype(jnp.bfloat16)
    grad_w_gate = matmul_left_t(normed_mlp_b, grad_gate_b)
    grad_w_up = matmul_left_t(normed_mlp_b, grad_up_b)
    grad_normed_mlp = matmul_right_t(grad_gate_b, weight_gate) + matmul_right_t(
        grad_up_b, weight_up
    )
    grad_middle, grad_gain_mlp = mlp_norm_back(grad_normed_mlp)
    grad_inputs = grad_inputs + grad_middle
    grad_attn_b = (grad_branch + grad_middle).astype(jnp.bfloat16)
    grad_w_out = matmul_left_t(mixed_b, grad_attn_b)
    grad_mixed = matmul_right_t(grad_attn_b, weight_out).astype(jnp.bfloat16)
    grad_heads = grad_mixed.reshape(row_count, kv_count, group_size, head_width).transpose(
        1, 0, 2, 3
    )

    def head_backward(packed):
        query_head, key_head, value_head, grad_head, log_head = packed
        raw_scores = (
            jnp.einsum("qgd,kd->gqk", query_head, key_head, preferred_element_type=jnp.float32)
            * score_scale
        )
        raw_scores = jnp.where(allowed[None], raw_scores, neg_big)
        probs = jnp.exp(raw_scores - log_head[..., None])
        grad_probs = jnp.einsum(
            "qgd,kd->gqk", grad_head, value_head, preferred_element_type=jnp.float32
        )
        row_delta = jnp.sum(probs * grad_probs, axis=-1, keepdims=True)
        grad_scores = (probs * (grad_probs - row_delta)).astype(jnp.bfloat16)
        grad_q = (
            jnp.einsum("gqk,kd->qgd", grad_scores, key_head, preferred_element_type=jnp.float32)
            * score_scale
        )
        grad_k = (
            jnp.einsum("gqk,qgd->kd", grad_scores, query_head, preferred_element_type=jnp.float32)
            * score_scale
        )
        grad_v = jnp.einsum(
            "gqk,qgd->kd", probs.astype(jnp.bfloat16), grad_head, preferred_element_type=jnp.float32
        )
        return (grad_q, grad_k, grad_v)

    grad_q_heads, grad_k_heads, grad_v_heads = lax.map(
        head_backward,
        (query_heads, split_heads(key_all), split_heads(value_all), grad_heads, log_totals),
    )
    grad_keys_all = grad_k_heads.transpose(1, 0, 2).reshape(total_rows, kv_width)
    grad_values_all = grad_v_heads.transpose(1, 0, 2).reshape(total_rows, kv_width)
    own_grad_keys, own_grad_values = (
        lax.psum_scatter(grad_keys_all, "ctx", scatter_dimension=0, tiled=True),
        lax.psum_scatter(grad_values_all, "ctx", scatter_dimension=0, tiled=True),
    )
    grad_query_b = (
        rotate(
            grad_q_heads.transpose(1, 0, 2, 3).reshape(row_count, head_count, head_width),
            cosine,
            -sine_table,
        )
        .astype(jnp.bfloat16)
        .reshape(row_count, model_width)
    )
    grad_key_b = (
        rotate(own_grad_keys.reshape(row_count, kv_count, head_width), cosine, -sine_table)
        .astype(jnp.bfloat16)
        .reshape(row_count, kv_width)
    )
    grad_value_b = own_grad_values.astype(jnp.bfloat16)
    grad_w_query = matmul_left_t(normed_b, grad_query_b)
    grad_w_key = matmul_left_t(normed_b, grad_key_b)
    grad_w_value = matmul_left_t(normed_b, grad_value_b)
    grad_normed = (
        matmul_right_t(grad_query_b, weight_query)
        + matmul_right_t(grad_key_b, weight_key)
        + matmul_right_t(grad_value_b, weight_value)
    )
    grad_in_norm, grad_gain_attn = norm_back(grad_normed)
    grad_inputs = grad_inputs + grad_in_norm
    query_shard, key_shard, value_shard, out_shard, gate_shard, up_shard, down_shard = (
        lax.psum_scatter(grad_w_query.reshape(-1), ("dp", "ctx"), scatter_dimension=0, tiled=True),
        lax.psum_scatter(grad_w_key.reshape(-1), ("dp", "ctx"), scatter_dimension=0, tiled=True),
        lax.psum_scatter(grad_w_value.reshape(-1), ("dp", "ctx"), scatter_dimension=0, tiled=True),
        lax.psum_scatter(grad_w_out.reshape(-1), ("dp", "ctx"), scatter_dimension=0, tiled=True),
        lax.psum_scatter(grad_w_gate.reshape(-1), ("dp", "ctx"), scatter_dimension=0, tiled=True),
        lax.psum_scatter(grad_w_up.reshape(-1), ("dp", "ctx"), scatter_dimension=0, tiled=True),
        lax.psum_scatter(grad_w_down.reshape(-1), ("dp", "ctx"), scatter_dimension=0, tiled=True),
    )
    gain_attn_sum, gain_mlp_sum, router_sum = lax.psum(
        (grad_gain_attn, grad_gain_mlp, grad_router), ("dp", "ctx")
    )
    return (
        result[None],
        grad_inputs.astype(jnp.bfloat16)[None],
        query_shard,
        key_shard,
        value_shard,
        out_shard,
        gate_shard,
        up_shard,
        down_shard,
        gain_attn_sum,
        gain_mlp_sum,
        router_sum,
    )


def solution(mesh):
    placed = (
        P("dp", "ctx", None),
        P("dp", "ctx", None),
        P("dp"),
        P("dp", "ctx"),
        P(),
        P(("dp", "ctx")),
        P(("dp", "ctx")),
        P(("dp", "ctx")),
        P(("dp", "ctx")),
        P(("dp", "ctx")),
        P(("dp", "ctx")),
        P(("dp", "ctx")),
        P(),
        P(),
        P(),
    )
    return jax.shard_map(
        per_device,
        mesh=mesh,
        in_specs=placed,
        out_specs=(
            P("dp", "ctx", None),
            P("dp", "ctx", None),
            P(("dp", "ctx")),
            P(("dp", "ctx")),
            P(("dp", "ctx")),
            P(("dp", "ctx")),
            P(("dp", "ctx")),
            P(("dp", "ctx")),
            P(("dp", "ctx")),
            P(),
            P(),
            P(),
        ),
        check_vma=False,
    )
```

profile of v0, /device:TPU:0, one launch (start us, length us, event | category | flops | bytes accessed | tf_op | source)
XLA Modules:
  0.0 1370.1 jit_solution(13818543416422502174)
XLA Ops:
  9.6 84.9 %all-gather = bf16[32,1,9600]{2,1,0:T(2,128)(2,1)S(1)} all-gather(bf16[1,1,9600]{2,1,0:T(2,128)(2,1)S(1)} %reshape.399), channel_id=1, replica_groups=mesh['dp'=8,'ctx'=4] {'dp','ctx'}, dimensions={0}, use_global_device_ids=true | all-gather | bytes 633600 | tf_op jit(solution)/shard_map/all_gather | solution.py:108
  101.7 81.8 %all-gather.1 = bf16[32,1,9600]{2,1,0:T(2,128)(2,1)S(1)} all-gather(bf16[1,1,9600]{2,1,0:T(2,128)(2,1)S(1)} %reshape.401), channel_id=1, replica_groups=mesh['dp'=8,'ctx'=4] {'dp','ctx'}, dimensions={0}, use_global_device_ids=true | all-gather | bytes 633600 | tf_op jit(solution)/shard_map/all_gather | solution.py:107
  196.9 40.8 %reduce.2 = bf16[32,28800]{1,0:T(8,128)(2,1)} reduce(bf16[32,1,28800]{2,1,0:T(2,128)(2,1)} %all-gather.22.cloned.1.call-done, bf16[]{:T(256)} %constant.108), dimensions={1}, to_apply=%all-gather.2.reduce_sub_computation | reduce | bytes 3686402 | tf_op jit(solution)/shard_map/all_gather | solution.py:106
  247.5 75.0 %while.30 = (s32[]{:T(128)}, bf16[5,512,3,64]{1,3,2,0:T(8,128)(2,1)}, f32[5,3,512]{2,1,0:T(4,128)S(1)}, bf16[5,2048,64]{1,2,0:T(8,128)(2,1)}, bf16[5,2048,64]{1,...) while((s32[]{:T(128)}, ...), condition=%wide.region_4.5_spmd.clone.clone, body=%wide.region_1.4_spmd.clone.sunk.clone | while | flops 845150720 | bytes 47321220 | solution.py:158
  249.3 3.9 fusion.203
  253.1 3.9 fusion.204
  257.0 5.7 fusion.205
  264.2 3.9 fusion.203
  268.1 3.9 fusion.204
  272.0 5.7 fusion.205
  279.2 3.9 fusion.203
  283.1 3.9 fusion.204
  287.0 5.6 fusion.205
  294.2 3.9 fusion.203
  298.1 3.9 fusion.204
  301.9 5.6 fusion.205
  309.1 3.9 fusion.203
  313.0 3.9 fusion.204
  316.9 5.6 fusion.205
  322.6 39.5 %reduce.3 = bf16[32,28800]{1,0:T(8,128)(2,1)S(1)} reduce(bf16[32,1,28800]{2,1,0:T(2,128)(2,1)} %all-gather.24.cloned.1.call-done, bf16[]{:T(256)} %constant.108), dimensions={1}, to_apply=%all-gather.3.reduce_sub_computation | reduce | bytes 3686402 | tf_op jit(solution)/shard_map/all_gather | solution.py:109
  369.9 10.3 reshape.383
  380.3 35.4 %all-gather.18.cloned.1.call-done = bf16[2457600]{0:T(1024)(128)(2,1)} async-done(((bf16[76800]{0:T(1024)(128)(2,1)}), bf16[2457600]{0:T(1024)(128)(2,1)}) %all-gather.18.cloned.1.call-update) | async-done | bytes 4915216 | tf_op jit(solution)/shard_map/all_gather | solution.py:111
  415.6 10.0 reshape.384
  425.6 7.2 fusion.122
  432.8 4.7 fusion.123
  437.5 43.6 %all-gather.20.cloned.1.call-done = bf16[2457600]{0:T(1024)(128)(2,1)} async-done(((bf16[76800]{0:T(1024)(128)(2,1)}), bf16[2457600]{0:T(1024)(128)(2,1)}) %all-gather.20.cloned.1.call-update) | async-done | bytes 4915216 | tf_op jit(solution)/shard_map/all_gather | solution.py:112
  481.1 9.5 reshape.385
  490.6 9.5 multiply_convert_fusion
  500.1 7.1 fusion.124
  507.3 6.3 multiply_reduce_fusion
  513.7 5.3 fusion.78
  520.9 145.6 %while.31 = (s32[]{:T(128)}, f32[5,512,3,64]{1,3,2,0:T(8,128)S(1)}, f32[5,2048,64]{1,2,0:T(8,128)}, f32[5,2048,64]{1,2,0:T(8,128)}, bf16[5,2048,64]{1,2,0:T(8,12...) while((s32[]{:T(128)}, f32[5,512,3,64]{1,3,2,0:T(8,128)S(1)}, ...), condition=%wide.region_10.11_spmd.clone.clone, body=%wide.region_8.10_spmd.clone.sunk.clone | while | flops 2062776832 | bytes 101645440 | solution.py:230
  525.4 7.7 fusion.215
  533.2 6.9 fusion.216
  545.9 4.2 fusion.219
  554.5 7.7 fusion.215
  562.2 6.9 fusion.216
  571.3 3.7 fusion.218
  575.0 4.2 fusion.219
  583.6 7.7 fusion.215
  591.3 6.9 fusion.216
  600.4 3.8 fusion.218
  604.1 4.2 fusion.219
  612.7 7.7 fusion.215
  620.4 6.9 fusion.216
  629.5 3.7 fusion.218
  633.2 4.2 fusion.219
  641.8 7.7 fusion.215
  649.5 6.9 fusion.216
  658.6 3.7 fusion.218
  662.3 4.2 fusion.219
  671.7 5.8 reshape.391
  677.6 4.3 fusion.125
  681.9 5.6 reshape.394
  687.5 7.0 fusion.126
  694.5 11.0 reshape.395
  705.5 7.0 fusion.127
  712.5 11.1 reshape.396
  723.6 7.6 fusion.91
  731.2 13.3 reshape.397
  748.3 23.1 %reduce-scatter.5.cloned.1.call-done = f32[512,320]{0,1:T(8,128)} async-done(((f32[2048,320]{0,1:T(8,128)}), f32[512,320]{0,1:T(8,128)}) %reduce-scatter.5.cloned.1.call-update) | async-done | bytes 655376 | tf_op jit(solution)/shard_map/reduce_scatter | solution.py:238
  782.9 41.8 %all-reduce.7 = (f32[960]{0:T(1024)}, f32[960]{0:T(1024)}, f32[960]{0:T(1024)}) all-reduce(f32[960]{0:T(1024)S(1)} %get-tuple-element.163, f32[960]{0:T(1024)S(1)} %copy-done.49, f32[960]{0:T(1024)S(1)} %bitcast.380), channel_id=1, replica_groups=mesh['dp'=8,'ctx'=4] {'dp','ctx'}, use_global_device_ids=true, to_apply=%region_22.23 | all-reduce | flops 2880 | bytes 23040 | tf_op jit(solution)/shard_map/psum | solution.py:274
  824.7 4.1 fusion.115
  828.8 522.8 %all-reduce.11.cloned.1.call-done = (f32[921600]{0:T(1024)}, f32[307200]{0:T(1024)}, f32[307200]{0:T(1024)}, f32[921600]{0:T(1024)}, f32[2457600]{0:T(1024)}, /*index=5*/f32[2457600]{0:T(1024)}, f32[2457600]{0:T(1024)}) async-done(((f32[921600]{0:T(1024)}, f32[307200]{0:T(1024)}, f32[307200]{0:T(1024)}, f32[921600]{0:T(1024)}, f32[2457600]{0:T(1024)}, /*index=5*/f32[2457600]{0:T(1024)}, f32[2457600]{0:T(1024)}), ...) | async-done | bytes 39321616
  (252 shorter events, 117.2 us)
Async XLA Ops:
  7.2 189.7 %all-gather.22.cloned.1.call-start = ((), (), s32[]{:S(2)}) async-start(), calls=%async_computation.9 | async-start | bytes 3801600 | tf_op jit(solution)/shard_map/all_gather | solution.py:106
  8.8 238.8 %all-gather.12.cloned.1.call-start = ((), (), s32[]{:S(2)}) async-start(), calls=%async_computation.2 | async-start | bytes 1638400 | tf_op jit(solution)/shard_map/all_gather | solution.py:137
  9.6 89.4 %copy-start.1 = (bf16[1,512,960]{1,2,0:T(8,128)(2,1)S(1)}, bf16[1,512,960]{1,2,0:T(8,128)(2,1)}, u32[]{:S(2)}) copy-start(bf16[1,512,960]{1,2,0:T(8,128)(2,1)} %param.19) | copy-start | bytes 2949124
  94.5 4.8 copy-start.28
  99.0 1.8 copy-start.14
  99.3 2.2 copy-start.35
  99.3 2.2 copy-start.54
  99.3 2.3 copy-start.32
  99.3 144.0 %copy-start.30 = (f32[512]{0:T(512)}, f32[512]{0:T(512)S(1)}, u32[]{:S(2)}) copy-start(f32[512]{0:T(512)S(1)} %fusion.119) | copy-start | bytes 6148
  100.8 146.7 %all-gather.14.cloned.1.call-start = ((), (), s32[]{:S(2)}) async-start(), calls=%async_computation.3 | async-start | bytes 1638400 | tf_op jit(solution)/shard_map/all_gather | solution.py:136
  188.0 2.5 copy-start.12
  189.9 56.3 %copy-start.20 = (f32[512,32]{0,1:T(8,128)}, f32[512,32]{0,1:T(8,128)S(1)}, u32[]{:S(2)}) copy-start(f32[512,32]{0,1:T(8,128)S(1)} %get-tuple-element.239) | copy-start | bytes 196612
  190.5 5.3 copy-start.52
  190.5 5.3 copy-start.41
  191.4 131.2 %all-gather.24.cloned.1.call-start = ((), (), s32[]{:S(2)}) async-start(), calls=%async_computation.10 | async-start | bytes 3801600 | tf_op jit(solution)/shard_map/all_gather | solution.py:109
  192.2 177.7 %all-gather.16.cloned.1.call-start = ((), (), s32[]{:S(2)}) async-start(), calls=%async_computation.4 | async-start | bytes 5068800 | tf_op jit(solution)/shard_map/all_gather | solution.py:110
  192.8 222.8 %all-gather.18.cloned.1.call-start = ((), (), s32[]{:S(2)}) async-start(), calls=%async_computation.5 | async-start | bytes 5068800 | tf_op jit(solution)/shard_map/all_gather | solution.py:111
  193.4 287.7 %all-gather.20.cloned.1.call-start = ((), (), s32[]{:S(2)}) async-start(), calls=%async_computation.6 | async-start | bytes 5068800 | tf_op jit(solution)/shard_map/all_gather | solution.py:112
  194.1 550.4 %reduce-scatter.3.cloned.1.call-start = ((), (), s32[]{:S(2)}) async-start(), calls=%async_computation.7 | async-start | bytes 3276800 | tf_op jit(solution)/shard_map/reduce_scatter | solution.py:237
  195.7 41.9 %copy-start.39 = (f32[1,512]{1,0:T(1,128)}, f32[1,512]{1,0:T(1,128)S(1)}, u32[]{:S(2)}) copy-start(f32[1,512]{1,0:T(1,128)S(1)} %convert_element_type.146) | copy-start | bytes 6148
  196.2 41.4 %copy-start.37 = (f32[1,512]{1,0:T(1,128)}, f32[1,512]{1,0:T(1,128)S(1)}, u32[]{:S(2)}) copy-start(f32[1,512]{1,0:T(1,128)S(1)} %fusion.107) | copy-start | bytes 6148
  240.7 2.7 copy-start.10
  249.2 3.9 copy-start
  264.2 3.9 copy-start
  279.2 3.9 copy-start
  294.2 3.9 copy-start
  309.1 3.9 copy-start
  362.1 3.0 copy-start.2
  365.1 4.4 copy-start.43
  368.2 1.3 copy-start.7
  368.3 145.4 %copy-start.33 = (f32[512]{0:T(512)}, f32[512]{0:T(512)S(1)}, u32[]{:S(2)}) copy-start(f32[512]{0:T(512)S(1)} %fusion.120) | copy-start | bytes 6148
  369.9 63.0 %copy-start.5 = (bf16[512,960]{0,1:T(8,128)(2,1)}, bf16[512,960]{0,1:T(8,128)(2,1)S(1)}, u32[]{:S(2)}) copy-start(bf16[512,960]{0,1:T(8,128)(2,1)S(1)} %multiply_convert_fusion.2) | copy-start | bytes 2949124
  425.6 7.3 copy-start.4
  437.5 53.1 %copy-start.22 = (bf16[1,512,960]{1,2,0:T(8,128)(2,1)S(1)}, bf16[1,512,960]{1,2,0:T(8,128)(2,1)}, u32[]{:S(2)}) copy-start(bf16[1,512,960]{1,2,0:T(8,128)(2,1)} %param.20) | copy-start | bytes 2949124
  437.5 53.1 %copy-start.45 = (f32[512]{0:T(512)S(1)}, f32[512]{0:T(512)}, u32[]{:S(2)}) copy-start(f32[512]{0:T(512)} %get-tuple-element.217) | copy-start | bytes 6148
  437.5 53.1 %copy-start.50 = (f32[512]{0:T(512)S(1)}, f32[512]{0:T(512)}, u32[]{:S(2)}) copy-start(f32[512]{0:T(512)} %fusion.121) | copy-start | bytes 6148
  500.1 7.2 copy-start.58
  500.1 7.2 copy-start.57
  500.1 13.5 copy-start.56
  500.1 7.1 copy-start.8
  500.1 13.5 slice-start
  507.3 6.4 slice-start.1
  513.6 5.4 copy-start.17
  513.6 5.4 copy-start.47
  513.7 5.3 copy-start.19
  519.0 1.9 copy-start.18
  666.6 104.9 %reduce-scatter.5.cloned.1.call-start = ((), (), s32[]{:S(2)}) async-start(), calls=%async_computation.8 | async-start | bytes 3276800 | tf_op jit(solution)/shard_map/reduce_scatter | solution.py:238
  667.3 684.4 %all-reduce.11.cloned.1.call-start = ((), (), s32[]{:S(2)}) async-start(), calls=%async_computation.11 | async-start | bytes 78643200
  667.8 3.9 copy-start.24
  671.7 5.8 copy-start.25
  681.9 5.6 copy-start.6
  712.5 11.1 copy-start.23
  712.5 11.1 copy-start.46
  712.5 11.1 copy-start.51
  775.1 1.6 copy-start.11
  776.6 2.5 copy-start.13
  779.1 1.3 copy-start.16
  780.4 2.4 copy-start.49
  780.4 44.2 %copy-start.36 = (f32[512]{0:T(512)S(1)}, f32[512]{0:T(512)}, u32[]{:S(2)}) copy-start(f32[512]{0:T(512)} %copy-done.35) | copy-start | bytes 6148
  780.4 44.3 %copy-start.9 = (f32[512,960]{0,1:T(8,128)S(1)}, f32[512,960]{0,1:T(8,128)}, u32[]{:S(2)}) copy-start(f32[512,960]{0,1:T(8,128)} %copy-done.7) | copy-start | bytes 5898244
  780.4 44.3 %copy-start.34 = (f32[512]{0:T(512)S(1)}, f32[512]{0:T(512)}, u32[]{:S(2)}) copy-start(f32[512]{0:T(512)} %copy-done.33) | copy-start | bytes 6148
  780.4 44.3 %copy-start.42 = (f32[960]{0:T(1024)S(1)}, f32[960]{0:T(1024)}, u32[]{:S(2)}) copy-start(f32[960]{0:T(1024)} %param.33) | copy-start | bytes 11524
  780.4 44.3 %copy-start.44 = (f32[960]{0:T(1024)S(1)}, f32[960]{0:T(1024)}, u32[]{:S(2)}) copy-start(f32[960]{0:T(1024)} %param.32) | copy-start | bytes 11524
  780.5 44.3 %copy-start.48 = (f32[512]{0:T(512)S(1)}, f32[512]{0:T(512)}, u32[]{:S(2)}) copy-start(f32[512]{0:T(512)} %copy-done.47) | copy-start | bytes 6148
  (11 other events, 10.7 us)
Sparse Core Ops, SparseCore 0:
  11.4 65.3 all-gather.21
  100.9 36.9 all-gather.11
  191.5 29.9 all-gather.13
  224.8 59.7 all-gather.23
  287.3 62.9 all-gather.15
  353.0 62.5 all-gather.17
  418.5 62.6 all-gather.19
  666.7 50.5 reduce-scatter.2
  719.6 51.7 reduce-scatter.4
  777.7 573.9 all-reduce.10
where the time goes:
time: 1380 us; the launch traced here: 1370 us
  waiting for transfers between devices  627 us (45%)
  matrix products  238 us (17%)
  blocking collectives  209 us (15%)
  other arithmetic  169 us (12%)
  local copies, waits for them, and re-layouts  110 us (8%)
  between operations  15.8 us (1%)
    unnamed x11, waiting for transfers between devices  525 us
    all_gather x1, blocking collectives, per_device(): lax.all_gather(w_value, ('dp', 'ctx'), axis=0, tiled=True)  84.9 us
    all_gather x1, blocking collectives, per_device(): lax.all_gather(w_key, ('dp', 'ctx'), axis=0, tiled=True)  81.8 us
    all_gather x1, waiting for transfers between devices, per_device(): lax.all_gather(w_down, ('dp', 'ctx'), axis=0, tiled=True)  43.6 us
    psum x1, blocking collectives, per_device(): lax.psum((grad_gain_attn, grad_gain_mlp, grad_router), ('dp', 'ctx'))  41.8 us
    all_gather x1, other arithmetic, per_device(): lax.all_gather(w_query, ('dp', 'ctx'), axis=0, tiled=True)  40.8 us
    all_gather x1, other arithmetic, per_device(): lax.all_gather(w_out, ('dp', 'ctx'), axis=0, tiled=True)  39.5 us
    dot_general x5, matrix products, head_backward(): jnp.einsum('qgd,kd->gqk', grad_head, value_head, preferred_element_type=j...  38.5 us
  transfers between devices with their start and end apart: 10, of which 4 were waited for; matrix products, arithmetic and copies ran while one was open for 23% of the time, Pallas kernels for 0%

commit v1 on v0

--- a/solution.py
+++ b/solution.py
@@ -11,6 +11,18 @@
 rope_base = 100000.0
 neg_big = -1e30
 highest = lax.Precision.HIGHEST
+
+
+def collect(array, axis, dim):
+    ways, here, lap = (lax.axis_size(axis), lax.axis_index(axis), array.shape[dim])
+    line, have = (array, 1)
+    while have < ways:
+        line = jnp.concatenate(
+            [line, lax.ppermute(line, axis, [(d, (d - have) % ways) for d in range(ways)])],
+            axis=dim,
+        )
+        have = 2 * have
+    return jnp.roll(line, here * lap, axis=dim)
 
 
 def rms_norm(values_in, gain_vec):
@@ -104,7 +116,7 @@
     )
     whole = (
         lax.all_gather(w_query, ("dp", "ctx"), axis=0, tiled=True),
-        lax.all_gather(w_key, ("dp", "ctx"), axis=0, tiled=True),
+        collect(w_key, ("dp", "ctx"), 0),
         lax.all_gather(w_value, ("dp", "ctx"), axis=0, tiled=True),
         lax.all_gather(w_out, ("dp", "ctx"), axis=0, tiled=True),
         lax.all_gather(w_gate, ("dp", "ctx"), axis=0, tiled=True),

time: 1380 us -> 1340 us (0.971)
  blocking collectives: 209 us -> 122 us
  local copies, waits for them, and re-layouts: 110 us -> 130 us
  waiting for transfers between devices: 627 us -> 643 us
    all_gather x1 -> x0, blocking collectives: 81.8 us -> none  [per_device(): lax.all_gather(w_key, ('dp', 'ctx'), axis=0, tiled=True)]
    unnamed x132 -> x145, local copies, waits for them, and re-layouts: 18.7 us -> 36.1 us
  transfers between devices with their start and end apart: 10 -> 15, of which waited for: 4 -> 7; matrix products, arithmetic and copies ran while one was open for 23% -> 25% of each run, Pallas kernels for 0% -> 0%
where the time goes in v1:
time: 1340 us; the launch traced here: 1320 us
  waiting for transfers between devices  643 us (48%)
  matrix products  238 us (18%)
  other arithmetic  166 us (12%)
  local copies, waits for them, and re-layouts  130 us (10%)
  blocking collectives  122 us (9%)
  between operations  16.1 us (1%)
    unnamed x11, waiting for transfers between devices  525 us
    all_gather x1, blocking collectives, per_device(): lax.all_gather(w_value, ('dp', 'ctx'), axis=0, tiled=True)  80.4 us
    all_gather x1, waiting for transfers between devices, per_device(): lax.all_gather(w_down, ('dp', 'ctx'), axis=0, tiled=True)  43.6 us
    psum x1, blocking collectives, per_device(): lax.psum((grad_gain_attn, grad_gain_mlp, grad_router), ('dp', 'ctx'))  41.8 us
    all_gather x1, other arithmetic, per_device(): lax.all_gather(w_query, ('dp', 'ctx'), axis=0, tiled=True)  40.8 us
    all_gather x1, other arithmetic, per_device(): lax.all_gather(w_out, ('dp', 'ctx'), axis=0, tiled=True)  39.5 us
    dot_general x5, matrix products, head_backward(): jnp.einsum('qgd,kd->gqk', grad_head, value_head, preferred_element_type=j...  38.5 us
    all_gather x1, waiting for transfers between devices, per_device(): lax.all_gather(w_up, ('dp', 'ctx'), axis=0, tiled=True)  38.3 us
  transfers between devices with their start and end apart: 15, of which 7 were waited for; matrix products, arithmetic and copies ran while one was open for 25% of the time, Pallas kernels for 0%

profile of v1, /device:TPU:0, one launch (start us, length us, event | category | flops | bytes accessed | tf_op | source)
XLA Modules:
  0.0 1324.2 jit_solution(10087319805093206161)
XLA Ops:
  8.8 6.5 collective-permute-start
  17.5 80.4 %all-gather = bf16[32,1,9600]{2,1,0:T(2,128)(2,1)S(1)} all-gather(bf16[1,1,9600]{2,1,0:T(2,128)(2,1)S(1)} %reshape.399), channel_id=1, replica_groups=mesh['dp'=8,'ctx'=4] {'dp','ctx'}, dimensions={0}, use_global_device_ids=true | all-gather | bytes 633600 | tf_op jit(solution)/shard_map/all_gather | solution.py:120
  122.0 7.4 collective-permute-done.4
  147.7 40.8 %reduce.1 = bf16[32,28800]{1,0:T(8,128)(2,1)} reduce(bf16[32,1,28800]{2,1,0:T(2,128)(2,1)} %all-gather.21.cloned.1.call-done, bf16[]{:T(256)} %constant.135), dimensions={1}, to_apply=%all-gather.1.reduce_sub_computation | reduce | bytes 3686402 | tf_op jit(solution)/shard_map/all_gather | solution.py:118
  198.3 75.0 %while.30 = (s32[]{:T(128)}, bf16[5,512,3,64]{1,3,2,0:T(8,128)(2,1)}, f32[5,3,512]{2,1,0:T(4,128)S(1)}, bf16[5,2048,64]{1,2,0:T(8,128)(2,1)}, bf16[5,2048,64]{1,...) while((s32[]{:T(128)}, ...), condition=%wide.region_4.5_spmd.clone.clone, body=%wide.region_1.4_spmd.clone.sunk.clone | while | flops 845150720 | bytes 47321220 | solution.py:170
  200.1 3.9 fusion.203
  203.9 3.9 fusion.204
  207.8 5.6 fusion.205
  215.0 3.9 fusion.203
  218.9 3.9 fusion.204
  222.8 5.6 fusion.205
  230.0 3.9 fusion.203
  233.9 3.9 fusion.204
  237.8 5.6 fusion.205
  245.0 3.9 fusion.203
  248.9 3.9 fusion.204
  252.7 5.7 fusion.205
  260.0 3.9 fusion.203
  263.8 3.9 fusion.204
  267.7 5.6 fusion.205
  273.4 39.5 %reduce.2 = bf16[32,28800]{1,0:T(8,128)(2,1)S(1)} reduce(bf16[32,1,28800]{2,1,0:T(2,128)(2,1)} %all-gather.23.cloned.1.call-done, bf16[]{:T(256)} %constant.135), dimensions={1}, to_apply=%all-gather.2.reduce_sub_computation | reduce | bytes 3686402 | tf_op jit(solution)/shard_map/all_gather | solution.py:121
  320.7 10.3 reshape.383
  331.0 38.3 %all-gather.17.cloned.1.call-done = bf16[2457600]{0:T(1024)(128)(2,1)} async-done(((bf16[76800]{0:T(1024)(128)(2,1)}), bf16[2457600]{0:T(1024)(128)(2,1)}) %all-gather.17.cloned.1.call-update) | async-done | bytes 4915216 | tf_op jit(solution)/shard_map/all_gather | solution.py:123
  369.4 10.0 reshape.384
  379.3 7.2 fusion.123
  386.6 4.7 fusion.124
  391.3 43.6 %all-gather.19.cloned.1.call-done = bf16[2457600]{0:T(1024)(128)(2,1)} async-done(((bf16[76800]{0:T(1024)(128)(2,1)}), bf16[2457600]{0:T(1024)(128)(2,1)}) %all-gather.19.cloned.1.call-update) | async-done | bytes 4915216 | tf_op jit(solution)/shard_map/all_gather | solution.py:124
  434.8 9.5 reshape.385
  444.4 9.5 multiply_convert_fusion
  453.9 7.1 fusion.125
  461.0 6.3 multiply_reduce_fusion
  467.4 5.3 fusion.78
  474.6 145.8 %while.31 = (s32[]{:T(128)}, f32[5,512,3,64]{1,3,2,0:T(8,128)S(1)}, f32[5,2048,64]{1,2,0:T(8,128)}, f32[5,2048,64]{1,2,0:T(8,128)}, bf16[5,2048,64]{1,2,0:T(8,12...) while((s32[]{:T(128)}, f32[5,512,3,64]{1,3,2,0:T(8,128)S(1)}, ...), condition=%wide.region_10.11_spmd.clone.clone, body=%wide.region_8.10_spmd.clone.sunk.clone | while | flops 2062776832 | bytes 101645440 | solution.py:242
  479.2 7.7 fusion.215
  486.9 6.9 fusion.216
  499.6 4.3 fusion.219
  508.3 7.7 fusion.215
  516.0 6.9 fusion.216
  525.1 3.7 fusion.218
  528.8 4.2 fusion.219
  537.4 7.7 fusion.215
  545.1 6.9 fusion.216
  557.9 4.2 fusion.219
  566.6 7.7 fusion.215
  574.3 6.9 fusion.216
  583.3 3.7 fusion.218
  587.0 4.2 fusion.219
  595.7 7.7 fusion.215
  603.4 6.9 fusion.216
  612.4 3.7 fusion.218
  616.2 4.2 fusion.219
  625.6 5.8 reshape.391
  631.4 4.3 fusion.126
  635.7 5.6 reshape.394
  641.3 7.1 fusion.127
  648.4 11.0 reshape.395
  659.3 7.1 fusion.128
  666.4 11.1 reshape.396
  677.5 7.5 fusion.91
  685.0 13.3 %reshape.397 = f32[2457600]{0:T(1024)} reshape(f32[2560,960]{1,0:T(8,128)} %fusion.91) | data formatting | bytes 19660800 | tf_op jit(solution)/shard_map/reshape | solution.py:284
  702.0 23.3 %reduce-scatter.5.cloned.1.call-done = f32[512,320]{0,1:T(8,128)} async-done(((f32[2048,320]{0,1:T(8,128)}), f32[512,320]{0,1:T(8,128)}) %reduce-scatter.5.cloned.1.call-update) | async-done | bytes 655376 | tf_op jit(solution)/shard_map/reduce_scatter | solution.py:250
  736.7 41.8 %all-reduce.7 = (f32[960]{0:T(1024)}, f32[960]{0:T(1024)}, f32[960]{0:T(1024)}) all-reduce(f32[960]{0:T(1024)S(1)} %get-tuple-element.163, f32[960]{0:T(1024)S(1)} %copy-done.49, f32[960]{0:T(1024)S(1)} %bitcast.380), channel_id=1, replica_groups=mesh['dp'=8,'ctx'=4] {'dp','ctx'}, use_global_device_ids=true, to_apply=%region_22.23 | all-reduce | flops 2880 | bytes 23040 | tf_op jit(solution)/shard_map/psum | solution.py:286
  778.5 4.1 fusion.115
  782.6 522.9 %all-reduce.11.cloned.1.call-done = (f32[921600]{0:T(1024)}, f32[307200]{0:T(1024)}, f32[307200]{0:T(1024)}, f32[921600]{0:T(1024)}, f32[2457600]{0:T(1024)}, /*index=5*/f32[2457600]{0:T(1024)}, f32[2457600]{0:T(1024)}) async-done(((f32[921600]{0:T(1024)}, f32[307200]{0:T(1024)}, f32[307200]{0:T(1024)}, f32[921600]{0:T(1024)}, f32[2457600]{0:T(1024)}, /*index=5*/f32[2457600]{0:T(1024)}, f32[2457600]{0:T(1024)}), ...) | async-done | bytes 39321616
  (281 shorter events, 144.1 us)
Async XLA Ops:
  7.2 140.5 %all-gather.21.cloned.1.call-start = ((), (), s32[]{:S(2)}) async-start(), calls=%async_computation.9 | async-start | bytes 3801600 | tf_op jit(solution)/shard_map/all_gather | solution.py:118
  8.8 189.6 %all-gather.11.cloned.1.call-start = ((), (), s32[]{:S(2)}) async-start(), calls=%async_computation.2 | async-start | bytes 1638400 | tf_op jit(solution)/shard_map/all_gather | solution.py:149
  8.8 93.6 %collective-permute-start = (bf16[9600]{0:T(1024)(128)(2,1)}, bf16[9600]{0:T(1024)(128)(2,1)S(1)}, u32[]{:S(2)}, u32[]{:S(2)}) collective-permute-start(bf16[9600]{0:T(1024)(128)(2,1)} %param.25), channel_id=1, source_target_pairs={{0,31},{1,0},{2,1},{3,2},{4,3},{5,4},{6,5},{7,6},{8,7},{9,8},{10,9... | collective-permute-start | bytes 57608 | tf_op jit(solution)/shard_map/ppermute | solution.py:21
  17.5 84.9 %copy-start.35 = (f32[512]{0:T(512)}, f32[512]{0:T(512)S(1)}, u32[]{:S(2)}) copy-start(f32[512]{0:T(512)S(1)} %fusion.84) | copy-start | bytes 6148
  17.5 84.9 %copy-start.26 = (bf16[9600]{0:T(1024)(128)(2,1)S(1)}, bf16[9600]{0:T(1024)(128)(2,1)}, u32[]{:S(2)}) copy-start(bf16[9600]{0:T(1024)(128)(2,1)} %param.25) | copy-start | bytes 57604
  17.5 85.0 %copy-start.1 = (bf16[1,512,960]{1,2,0:T(8,128)(2,1)S(1)}, bf16[1,512,960]{1,2,0:T(8,128)(2,1)}, u32[]{:S(2)}) copy-start(bf16[1,512,960]{1,2,0:T(8,128)(2,1)} %param.19) | copy-start | bytes 2949124
  17.5 85.0 %copy-start.29 = (f32[960]{0:T(1024)S(1)}, f32[960]{0:T(1024)}, u32[]{:S(2)}) copy-start(f32[960]{0:T(1024)} %param.31) | copy-start | bytes 11524
  97.9 96.3 %copy-start.31 = (f32[512]{0:T(512)}, f32[512]{0:T(512)S(1)}, u32[]{:S(2)}) copy-start(f32[512]{0:T(512)S(1)} %fusion.120) | copy-start | bytes 6148
  102.4 7.2 copy-start.14
  102.4 5.1 copy-start.54
  102.5 4.9 collective-permute-start.1
  104.0 94.3 %all-gather.13.cloned.1.call-start = ((), (), s32[]{:S(2)}) async-start(), calls=%async_computation.3 | async-start | bytes 1638400 | tf_op jit(solution)/shard_map/all_gather | solution.py:148
  107.4 2.1 collective-permute-start.2
  109.6 10.8 collective-permute-start.3
  121.0 8.3 collective-permute-start.4
  122.0 75.0 %copy-start.20 = (f32[512,32]{0,1:T(8,128)}, f32[512,32]{0,1:T(8,128)S(1)}, u32[]{:S(2)}) copy-start(f32[512,32]{0,1:T(8,128)S(1)} %get-tuple-element.241) | copy-start | bytes 196612
  141.4 5.2 copy-start.52
  141.4 5.2 copy-start.41
  142.3 131.1 %all-gather.23.cloned.1.call-start = ((), (), s32[]{:S(2)}) async-start(), calls=%async_computation.10 | async-start | bytes 3801600 | tf_op jit(solution)/shard_map/all_gather | solution.py:121
  143.1 177.6 %all-gather.15.cloned.1.call-start = ((), (), s32[]{:S(2)}) async-start(), calls=%async_computation.4 | async-start | bytes 5068800 | tf_op jit(solution)/shard_map/all_gather | solution.py:122
  143.7 225.7 %all-gather.17.cloned.1.call-start = ((), (), s32[]{:S(2)}) async-start(), calls=%async_computation.5 | async-start | bytes 5068800 | tf_op jit(solution)/shard_map/all_gather | solution.py:123
  144.2 290.6 %all-gather.19.cloned.1.call-start = ((), (), s32[]{:S(2)}) async-start(), calls=%async_computation.6 | async-start | bytes 5068800 | tf_op jit(solution)/shard_map/all_gather | solution.py:124
  145.0 553.3 %reduce-scatter.3.cloned.1.call-start = ((), (), s32[]{:S(2)}) async-start(), calls=%async_computation.7 | async-start | bytes 3276800 | tf_op jit(solution)/shard_map/reduce_scatter | solution.py:249
  146.6 41.9 %copy-start.39 = (f32[1,512]{1,0:T(1,128)}, f32[1,512]{1,0:T(1,128)S(1)}, u32[]{:S(2)}) copy-start(f32[1,512]{1,0:T(1,128)S(1)} %convert_element_type.146) | copy-start | bytes 6148
  147.1 41.4 %copy-start.37 = (f32[1,512]{1,0:T(1,128)}, f32[1,512]{1,0:T(1,128)S(1)}, u32[]{:S(2)}) copy-start(f32[1,512]{1,0:T(1,128)S(1)} %fusion.107) | copy-start | bytes 6148
  191.5 2.7 copy-start.10
  200.0 3.9 copy-start
  215.0 3.9 copy-start
  230.0 3.9 copy-start
  245.0 3.9 copy-start
  260.0 3.9 copy-start
  312.9 3.0 copy-start.2
  315.9 4.4 copy-start.43
  319.1 148.3 %copy-start.33 = (f32[512]{0:T(512)}, f32[512]{0:T(512)S(1)}, u32[]{:S(2)}) copy-start(f32[512]{0:T(512)S(1)} %fusion.121) | copy-start | bytes 6148
  320.7 65.9 %copy-start.5 = (bf16[512,960]{0,1:T(8,128)(2,1)}, bf16[512,960]{0,1:T(8,128)(2,1)S(1)}, u32[]{:S(2)}) copy-start(bf16[512,960]{0,1:T(8,128)(2,1)S(1)} %multiply_convert_fusion.2) | copy-start | bytes 2949124
  379.3 7.2 copy-start.4
  391.2 53.1 %copy-start.22 = (bf16[1,512,960]{1,2,0:T(8,128)(2,1)S(1)}, bf16[1,512,960]{1,2,0:T(8,128)(2,1)}, u32[]{:S(2)}) copy-start(bf16[1,512,960]{1,2,0:T(8,128)(2,1)} %param.20) | copy-start | bytes 2949124
  391.3 53.1 %copy-start.45 = (f32[512]{0:T(512)S(1)}, f32[512]{0:T(512)}, u32[]{:S(2)}) copy-start(f32[512]{0:T(512)} %get-tuple-element.217) | copy-start | bytes 6148
  391.3 53.1 %copy-start.50 = (f32[512]{0:T(512)S(1)}, f32[512]{0:T(512)}, u32[]{:S(2)}) copy-start(f32[512]{0:T(512)} %fusion.122) | copy-start | bytes 6148
  453.8 7.2 copy-start.58
  453.8 7.2 copy-start.57
  453.9 13.5 %copy-start.56 = (bf16[512,2560]{1,0:T(8,128)(2,1)}, bf16[512,2560]{1,0:T(8,128)(2,1)S(1)}, u32[]{:S(2)}) copy-start(bf16[512,2560]{1,0:T(8,128)(2,1)S(1)} %get-tuple-element.225) | copy-start | bytes 7864324
  453.9 7.1 copy-start.8
  453.9 13.5 %slice-start = ((s8[5242880]{0:T(1024)(128)(4,1)}), s8[4194304]{0:T(1024)(128)(4,1)S(1)}, s32[]{:S(2)}) async-start(s8[5242880]{0:T(1024)(128)(4,1)} %bitcast.352), calls=%async_computation.12 | async-start | bytes 8388608
  461.0 6.4 slice-start.1
  467.3 5.4 copy-start.17
  467.3 5.4 copy-start.47
  467.4 5.3 copy-start.19
  620.4 104.9 %reduce-scatter.5.cloned.1.call-start = ((), (), s32[]{:S(2)}) async-start(), calls=%async_computation.8 | async-start | bytes 3276800 | tf_op jit(solution)/shard_map/reduce_scatter | solution.py:250
  621.2 684.4 %all-reduce.11.cloned.1.call-start = ((), (), s32[]{:S(2)}) async-start(), calls=%async_computation.11 | async-start | bytes 78643200
  621.7 3.9 copy-start.24
  625.6 5.8 copy-start.25
  635.7 5.6 copy-start.6
  666.4 11.1 copy-start.23
  666.4 11.1 copy-start.46
  666.4 11.1 copy-start.51
  730.5 2.5 copy-start.15
  730.5 2.5 copy-start.16
  734.2 44.3 %copy-start.36 = (f32[512]{0:T(512)S(1)}, f32[512]{0:T(512)}, u32[]{:S(2)}) copy-start(f32[512]{0:T(512)} %copy-done.35) | copy-start | bytes 6148
  734.2 44.3 %copy-start.9 = (f32[512,960]{0,1:T(8,128)S(1)}, f32[512,960]{0,1:T(8,128)}, u32[]{:S(2)}) copy-start(f32[512,960]{0,1:T(8,128)} %copy-done.7) | copy-start | bytes 5898244
  734.2 44.3 %copy-start.34 = (f32[512]{0:T(512)S(1)}, f32[512]{0:T(512)}, u32[]{:S(2)}) copy-start(f32[512]{0:T(512)} %copy-done.33) | copy-start | bytes 6148
  734.2 44.3 %copy-start.42 = (f32[960]{0:T(1024)S(1)}, f32[960]{0:T(1024)}, u32[]{:S(2)}) copy-start(f32[960]{0:T(1024)} %param.33) | copy-start | bytes 11524
  734.2 44.3 %copy-start.44 = (f32[960]{0:T(1024)S(1)}, f32[960]{0:T(1024)}, u32[]{:S(2)}) copy-start(f32[960]{0:T(1024)} %param.32) | copy-start | bytes 11524
  734.2 44.3 %copy-start.48 = (f32[512]{0:T(512)S(1)}, f32[512]{0:T(512)}, u32[]{:S(2)}) copy-start(f32[512]{0:T(512)} %copy-done.47) | copy-start | bytes 6148
  (16 other events, 18.7 us)
Sparse Core Ops, SparseCore 0:
  11.4 65.4 all-gather.20
  104.1 31.2 all-gather.10
  142.4 32.8 all-gather.12
  178.6 59.7 all-gather.22
  241.1 62.9 all-gather.14
  306.7 62.6 all-gather.16
  372.2 62.6 all-gather.18
  620.5 50.5 reduce-scatter.2
  673.5 51.7 reduce-scatter.4
  731.6 573.9 all-reduce.10
